TPU v7x, 32 devices: a whole 2x2x4 slice. The times are simulated.
32 devices in a mesh: dp: 8 (over y, x, core), fsdp: 4 (over z).
Axes of the slice: x: 2, y: 2, z: 4, core: 2. Of those that a mesh axis runs over, the one named last changes fastest.
Arguments:
- img_emb: bfloat16 [1024, 1024], P(('dp', 'fsdp')), may hold values from -0.25 to 0.25
- txt_emb: bfloat16 [1024, 1024], P(('dp', 'fsdp')), may hold values from -0.25 to 0.25
- img_ids: int32 [1024], P(('dp', 'fsdp')), may hold values from 0 to 1023
- txt_ids: int32 [1024], P(('dp', 'fsdp')), may hold values from 0 to 1023
- temp_log: float32 [1], replicated, may hold values from 1.5 to 2.5
- logit_bias: float32 [1], replicated, may hold values from -6 to -2
- block_in: bfloat16 [2048, 3072], P(('dp', 'fsdp')), may hold values from -6 to 6
- dw_kernel: float32 [49, 3072], replicated, may hold values from -0.875 to 0.875
- ln_gain: float32 [3072], replicated, may hold values from 0.5 to 1.5
- ln_bias: float32 [3072], replicated, may hold values from -3 to 3
- w_up: bfloat16 [3072, 6144], P(None, 'fsdp'), may hold values from -0.109375 to 0.109375
- w_down: bfloat16 [6144, 3072], P('fsdp'), may hold values from -0.078125 to 0.078125
- layer_scale: float32 [3072], replicated, may hold values from 0.1 to 1
- head_gain: float32 [3072], replicated, may hold values from 0.5 to 1.5
- head_bias: float32 [3072], replicated, may hold values from -3 to 3
- w_proj: bfloat16 [3072, 1024], replicated, may hold values from -0.109375 to 0.109375
Outputs:
- img_grad: float32 [1024, 1024], P(('dp', 'fsdp'))
- txt_grad: float32 [1024, 1024], P(('dp', 'fsdp'))
- w_up_grad: float32 [3072, 6144], P('dp', 'fsdp')
- w_down_grad: float32 [6144, 3072], P('fsdp', 'dp')
All inputs are finite; a program needn't handle non-finite values.
Results may differ from a plain program's by a relative error of at most 0.02.
Values may be sent and summed in bfloat16 or wider, within the bound.
A program may use at most 128 MiB of HBM per device.

v0:
```python
import jax
import jax.numpy as jnp
from jax import lax
from jax.sharding import PartitionSpec as P

KERNEL = 7
SIDE = 8


def unit_rows(matrix):
    values = matrix.astype(jnp.float32)
    length = jnp.sqrt(jnp.sum(values * values, axis=1, keepdims=True) + 1e-06)
    return (values / length, length)


def back_unit(gradient, unit_part, length):
    inner_prod = jnp.sum(unit_part * gradient, axis=1, keepdims=True)
    return (gradient - unit_part * inner_prod) / length


def pair_tile(images, image_ids, text_rows, text_ids, temper, offset):
    scores = jnp.dot(images, text_rows.T, preferred_element_type=jnp.float32)
    logits = temper * scores + offset
    labels = jnp.where(image_ids[:, None] == text_ids[None, :], 1.0, -1.0)
    weights = (temper * -labels * jax.nn.sigmoid(-labels * logits)).astype(jnp.bfloat16)
    image_part = jnp.dot(weights, text_rows, preferred_element_type=jnp.float32)
    text_part = jnp.dot(weights.T, images, preferred_element_type=jnp.float32)
    return (image_part, text_part)


def depthwise(pictures, kernel):
    reach = KERNEL // 2
    padded = jnp.pad(pictures, ((0, 0), (reach, reach), (reach, reach), (0, 0)))
    summed = jnp.zeros_like(pictures)
    for above in range(KERNEL):
        for across in range(KERNEL):
            summed = (
                summed
                + kernel[above * KERNEL + across]
                * padded[:, above : above + SIDE, across : across + SIDE, :]
            )
    return summed


def layer_norm(values, gain_vec, bias_vec):
    centre = jnp.mean(values, axis=-1, keepdims=True)
    centred = values - centre
    inverse = 1.0 / jnp.sqrt(jnp.mean(centred * centred, axis=-1, keepdims=True) + 1e-06)
    normal = centred * inverse
    return (normal * gain_vec + bias_vec, normal, inverse)


def head_back(patch_means, block_mean, image_sum, layer_scale, head_gain, head_bias, w_proj):
    pooled = patch_means.astype(jnp.float32) + layer_scale * block_mean
    head_out, head_norm, inverse = layer_norm(pooled, head_gain, head_bias)
    embed = jnp.dot(head_out.astype(jnp.bfloat16), w_proj, preferred_element_type=jnp.float32)
    embed_unit, embed_len = unit_rows(embed)
    embed_grad = back_unit(image_sum, embed_unit, embed_len).astype(jnp.bfloat16)
    head_grad = jnp.dot(embed_grad, w_proj.T, preferred_element_type=jnp.float32)
    norm_grad = head_grad * head_gain
    pool_grad = inverse * (
        norm_grad
        - jnp.mean(norm_grad, axis=1, keepdims=True)
        - head_norm * jnp.mean(norm_grad * head_norm, axis=1, keepdims=True)
    )
    return (layer_scale * pool_grad / (SIDE * SIDE)).astype(jnp.bfloat16)


def on_device(
    img_emb,
    txt_emb,
    img_ids,
    txt_ids,
    temp_log,
    logit_bias,
    block_in,
    dw_kernel,
    ln_gain,
    ln_bias,
    w_up,
    w_down,
    layer_scale,
    head_gain,
    head_bias,
    w_proj,
):
    channels = block_in.shape[1]
    hid_width = w_up.shape[1]
    temper = jnp.exp(temp_log[0])
    offset = logit_bias[0]
    img_unit, img_len = unit_rows(img_emb)
    txt_unit, txt_len = unit_rows(txt_emb)
    img_b = img_unit.astype(jnp.bfloat16)
    txt_b = txt_unit.astype(jnp.bfloat16)
    pictures = block_in.astype(jnp.float32).reshape(1, SIDE, SIDE, channels)
    mixed_rows = depthwise(pictures, dw_kernel).reshape(SIDE * SIDE, channels)
    normed = layer_norm(mixed_rows, ln_gain, ln_bias)[0].astype(jnp.bfloat16)
    patch_means = jnp.mean(pictures, axis=(1, 2)).astype(jnp.bfloat16)
    group_img, group_ids, group_normed = (
        lax.all_gather(img_b, "fsdp", axis=0, tiled=True),
        lax.all_gather(img_ids, "fsdp", axis=0, tiled=True),
        lax.all_gather(normed, "fsdp", axis=0, tiled=True),
    )
    image_count = group_normed.shape[0] // (SIDE * SIDE)
    image_part, text_part = pair_tile(
        group_img,
        group_ids,
        lax.all_gather(txt_b, "dp", axis=0, tiled=True),
        lax.all_gather(txt_ids, "dp", axis=0, tiled=True),
        temper,
        offset,
    )
    image_acc = image_part
    image_acc = lax.optimization_barrier(image_acc.astype(jnp.bfloat16)).astype(jnp.float32)
    hidden = jnp.dot(group_normed, w_up, preferred_element_type=jnp.float32)
    active = jax.nn.gelu(hidden).astype(jnp.bfloat16)
    active_total = jnp.sum(
        active.astype(jnp.float32).reshape(image_count, SIDE * SIDE, hid_width), axis=1
    )
    down_wide = w_down.astype(jnp.float32)
    partial_mean = jnp.dot(active_total / (SIDE * SIDE), down_wide, precision=lax.Precision.HIGHEST)
    image_sum, block_mean = (
        lax.psum_scatter(
            image_acc.astype(jnp.bfloat16), "fsdp", scatter_dimension=0, tiled=True
        ).astype(jnp.float32),
        lax.psum_scatter(
            partial_mean.astype(jnp.bfloat16), "fsdp", scatter_dimension=0, tiled=True
        ).astype(jnp.float32),
    )
    grad_row = head_back(
        patch_means, block_mean, image_sum[:1], layer_scale, head_gain, head_bias, w_proj
    )
    group_grad = lax.all_gather(grad_row, "fsdp", axis=0, tiled=True)
    row_down = jnp.dot(group_grad, w_down.T, preferred_element_type=jnp.float32)
    down_grad = jnp.broadcast_to(
        row_down[:, None, :], (image_count, SIDE * SIDE, hid_width)
    ).reshape(-1, hid_width)
    _, pullback = jax.vjp(jax.nn.gelu, hidden)
    hid_grad = pullback(down_grad)[0].astype(jnp.bfloat16)
    down_part = jnp.dot(
        active_total.T, group_grad.astype(jnp.float32), precision=lax.Precision.HIGHEST
    )
    up_part = jnp.dot(group_normed.T, hid_grad, preferred_element_type=jnp.float32)
    w_up_grad, w_down_grad, text_sum = (
        lax.psum_scatter(
            up_part.astype(jnp.bfloat16), "dp", scatter_dimension=0, tiled=True
        ).astype(jnp.float32),
        lax.psum_scatter(
            down_part.astype(jnp.bfloat16), "dp", scatter_dimension=1, tiled=True
        ).astype(jnp.float32),
        lax.psum_scatter(
            text_part.astype(jnp.bfloat16), "dp", scatter_dimension=0, tiled=True
        ).astype(jnp.float32),
    )
    img_grad = back_unit(image_sum, img_unit, img_len)
    txt_grad = back_unit(text_sum, txt_unit, txt_len)
    return (img_grad, txt_grad, w_up_grad, w_down_grad)


def solution(mesh):
    in_specs = (
        P(("dp", "fsdp"), None),
        P(("dp", "fsdp"), None),
        P(("dp", "fsdp")),
        P(("dp", "fsdp")),
        P(),
        P(),
        P(("dp", "fsdp"), None),
        P(),
        P(),
        P(),
        P(None, "fsdp"),
        P("fsdp", None),
        P(),
        P(),
        P(),
        P(),
    )
    out_specs = (P(("dp", "fsdp"), None), P(("dp", "fsdp"), None), P("dp", "fsdp"), P("fsdp", "dp"))
    return jax.shard_map(
        on_device, mesh=mesh, in_specs=in_specs, out_specs=out_specs, check_vma=False
    )
```

profile of v0, /device:TPU:0, one launch (start us, length us, event | category | flops | bytes accessed | tf_op | source)
XLA Modules:
  0.0 363.6 jit_solution(8530367770583388540)
XLA Ops:
  10.4 1.4 fusion.155
  15.3 9.9 %all-reduce.1 = s32[128]{0:T(128)S(1)} all-reduce(s32[128]{0:T(128)S(1)} %dynamic-update-slice), channel_id=1, replica_groups=mesh['dp'=8,'fsdp'=4] {'fsdp'}, use_global_device_ids=true, to_apply=%add.1 | all-reduce | flops 128 | bytes 1024
  26.1 8.0 %all-reduce.2 = s32[256]{0:T(256)S(1)} all-reduce(s32[256]{0:T(256)S(1)} %dynamic-update-slice.1), channel_id=1, replica_groups=mesh['dp'=8,'fsdp'=4] {'dp'}, use_global_device_ids=true, to_apply=%add.2 | all-reduce | flops 256 | bytes 2048
  35.9 14.2 %all_gather.20 = bf16[128,1024]{1,0:T(8,128)(2,1)S(1)} all-gather(bf16[32,1024]{1,0:T(8,128)(2,1)S(1)} %fusion.145), channel_id=1, replica_groups=mesh['dp'=8,'fsdp'=4] {'fsdp'}, dimensions={0}, use_global_device_ids=true | all-gather | bytes 327680 | tf_op jit(solution)/shard_map/all_gather | solution.py:100
  50.2 9.0 %all_gather.21 = bf16[256,1024]{1,0:T(8,128)(2,1)S(1)} all-gather(bf16[32,1024]{1,0:T(8,128)(2,1)S(1)} %fusion.146), channel_id=1, replica_groups=mesh['dp'=8,'fsdp'=4] {'dp'}, dimensions={0}, use_global_device_ids=true | all-gather | bytes 589824 | tf_op jit(solution)/shard_map/all_gather | solution.py:108
  61.1 5.5 %fusion.150 = (f32[8,8]{1,0:T(8,128)S(1)}, f32[1,8,8,3072]{3,2,1,0:T(8,128)S(1)}) fusion(f32[3072]{0:T(1024)S(1)} %bitcast.138, f32[3072]{0:T(1024)S(1)} %bitcast.139, f32[3072]{0:T(1024)S(1)} %bitcast.142, f32[3072]{0:T(1024)S(1)} %bitcast.143, f32[3072]{0:T(1024)S(1)} %bitcast.144, f32[3072]{0:T(1024)S(1)} %bitcast.145, f32[3072]{0:T(1024)S(1)} %bitcast.146, ...), kind=kLoop, calls=%fused_computation.236 | loop fusion | flops 19267520 | bytes 2175232 | tf_op jit(solution)/shard_map/reduce_sum | solution.py:46
  69.3 10.2 %reduce-scatter.7.cloned.1.call-done = bf16[32,1024]{1,0:T(8,128)(2,1)} async-done(((bf16[128,1024]{1,0:T(8,128)(2,1)}), bf16[32,1024]{1,0:T(8,128)(2,1)}) %reduce-scatter.7.cloned.1.call-update) | async-done | bytes 65552 | tf_op jit(solution)/shard_map/reduce_scatter | solution.py:123
  80.4 36.6 %all-gather.3.cloned.1.call-done = bf16[256,3072]{1,0:T(8,128)(2,1)} async-done(((bf16[64,3072]{1,0:T(8,128)(2,1)}), bf16[256,3072]{1,0:T(8,128)(2,1)}) %all-gather.3.cloned.1.call-update) | async-done | bytes 1572880 | tf_op jit(solution)/shard_map/all_gather | solution.py:102
  117.0 5.9 %convert_reduce_fusion = (f32[4,1536]{1,0:T(4,128)S(1)}, f32[256,1536]{1,0:T(8,128)S(1)}) fusion(bf16[256,3072]{1,0:T(8,128)(2,1)} %all-gather.3.cloned.1.call-done, bf16[3072,1536]{1,0:T(8,128)(2,1)} %param.26), kind=kOutput, calls=%fused_computation.65 | convolution fusion | flops 2420238336 | bytes 12607488 | tf_op jit(solution)/shard_map/dot_general | solution.py:115
  122.9 6.3 %convolution_convert_fusion.2 = bf16[4,3072]{1,0:T(4,128)(2,1)S(1)} fusion(bf16[1536,3072]{1,0:T(8,128)(2,1)} %param.27, f32[4,1536]{1,0:T(4,128)S(1)} %get-tuple-element.61), kind=kOutput, calls=%fused_computation.50 | convolution fusion | flops 226510848 | bytes 9486336 | tf_op jit(solution)/shard_map/dot_general | solution.py:121
  129.2 16.9 %all-reduce.3 = bf16[4,3072]{1,0:T(4,128)(2,1)S(1)} all-reduce(bf16[4,3072]{1,0:T(4,128)(2,1)S(1)} %convolution_convert_fusion.2), channel_id=4, replica_groups=mesh['dp'=8,'fsdp'=4] {'fsdp'}, use_global_device_ids=true, to_apply=%region_10.11.clone | all-reduce | flops 12288 | bytes 49152
  149.4 3.7 %fusion.126 = f32[1,1024]{1,0:T(1,128)S(1)} fusion(bf16[3072,1024]{1,0:T(8,128)(2,1)} %param.31, f32[1,3072]{1,0:T(1,128)S(1)} %bitcast.186, f32[1,3072]{1,0:T(1,128)S(1)} %bitcast.183, f32[1,3072]{1,0:T(1,128)S(1)} %get-tuple-element.7, f32[]{:T(128)S(6)} %sqrt.32, f32[]{:T(128)S(6)} %div.98), kind=kOutput, calls=%fused_computation.198 | convolution fusion | flops 6306816 | bytes 6332424 | tf_op jit(solution)/shard_map/dot_general | solution.py:56
  155.7 4.5 %fusion.137 = f32[1,3072]{1,0:T(1,128)S(1)} fusion(bf16[3072,1024]{1,0:T(8,128)(2,1)} %param.31, f32[1,1024]{1,0:T(1,128)S(1)} %bitcast.184, f32[32,1024]{1,0:T(8,128)S(1)} %convert_element_type.105, f32[]{:T(128)S(6)} %sqrt.33), kind=kOutput, calls=%fused_computation.216 | convolution fusion | flops 6294528 | bytes 6311940 | tf_op jit(solution)/shard_map/dot_general | solution.py:59
  162.8 13.3 %all-gather = bf16[4,1,3072]{2,1,0:T(2,128)(2,1)S(1)} all-gather(bf16[1,1,3072]{2,1,0:T(2,128)(2,1)S(1)} %convert_bitcast_fusion.1), channel_id=1, replica_groups=mesh['dp'=8,'fsdp'=4] {'fsdp'}, dimensions={0}, use_global_device_ids=true | all-gather | bytes 30720 | tf_op jit(solution)/shard_map/all_gather | solution.py:133
  176.1 9.7 %convolution_convert_fusion = bf16[1536,3072]{1,0:T(8,128)(2,1)} fusion(f32[4,1536]{1,0:T(4,128)S(1)} %get-tuple-element.61, bf16[4,1,3072]{2,1,0:T(2,128)(2,1)S(1)} %all-gather), kind=kOutput, calls=%fused_computation.48 | convolution fusion | flops 231211008 | bytes 9486336 | tf_op jit(solution)/shard_map/dot_general | solution.py:140
  185.8 12.7 %copy.20 = bf16[1536,3072]{0,1:T(8,128)(2,1)} copy(bf16[1536,3072]{1,0:T(8,128)(2,1)} %convolution_convert_fusion) | data formatting | bytes 18874368
  198.6 6.2 %fusion.123 = f32[4,1536]{1,0:T(4,128)S(1)} fusion(bf16[1536,3072]{1,0:T(8,128)(2,1)} %param.27, bf16[4,1,3072]{2,1,0:T(2,128)(2,1)S(1)} %all-gather), kind=kOutput, calls=%fused_computation.195 | convolution fusion | flops 37748736 | bytes 9486336 | tf_op jit(solution)/shard_map/dot_general | solution.py:134
  206.6 6.4 %convolution_convert_fusion.1 = bf16[3072,1536]{1,0:T(8,128)(2,1)} fusion(bf16[256,3072]{1,0:T(8,128)(2,1)S(1)} %copy-done, bf16[256,1536]{1,0:T(8,128)(2,1)S(1)} %fusion.6), kind=kOutput, calls=%fused_computation.49 | convolution fusion | flops 2420637696 | bytes 11796480 | tf_op jit(solution)/shard_map/dot_general | solution.py:143
  215.8 1.6 fusion.121
  217.4 56.5 %reduce-scatter.13.cloned.1.call-done = bf16[384,1536]{1,0:T(8,128)(2,1)} async-done(((bf16[3072,1536]{1,0:T(8,128)(2,1)}), bf16[384,1536]{1,0:T(8,128)(2,1)}) %reduce-scatter.13.cloned.1.call-update) | async-done | bytes 1179664
  273.9 1.7 copy.21
  275.6 1.6 convert_element_type.123
  277.2 76.9 %reduce-scatter.11.cloned.1.call-done = bf16[384,1536]{1,0:T(8,128)(2,1)} async-done(((bf16[3072,1536]{1,0:T(8,128)(2,1)}), bf16[384,1536]{1,0:T(8,128)(2,1)}) %reduce-scatter.11.cloned.1.call-update) | async-done | bytes 1179664 | tf_op jit(solution)/shard_map/reduce_scatter | solution.py:145
  354.1 3.0 convert_element_type.121
  (74 shorter events, 22.0 us)
Async XLA Ops:
  7.2 72.4 %reduce-scatter.7.cloned.1.call-start = ((), (), s32[]{:S(2)}) async-start(), calls=%async_computation.4 | async-start | bytes 327680 | tf_op jit(solution)/shard_map/reduce_scatter | solution.py:123
  50.2 10.3 %copy-start.5 = (f32[49,3072]{1,0:T(8,128)S(1)}, f32[49,3072]{1,0:T(8,128)}, u32[]{:S(2)}) copy-start(f32[49,3072]{1,0:T(8,128)} %param.23) | copy-start | bytes 1806340
  59.2 1.8 copy-start.1
  60.5 56.5 %all-gather.3.cloned.1.call-start = ((), (), s32[]{:S(2)}) async-start(), calls=%async_computation.6 | async-start | bytes 1966080 | tf_op jit(solution)/shard_map/all_gather | solution.py:102
  61.0 6.0 %copy-start.8 = (f32[3072]{0:T(1024)S(1)}, f32[3072]{0:T(1024)}, u32[]{:S(2)}) copy-start(f32[3072]{0:T(1024)} %param.25) | copy-start | bytes 36868
  61.1 5.9 %copy-start.9 = (f32[3072]{0:T(1024)S(1)}, f32[3072]{0:T(1024)}, u32[]{:S(2)}) copy-start(f32[3072]{0:T(1024)} %param.24) | copy-start | bytes 36868
  68.0 146.8 %reduce-scatter.9.cloned.1.call-start = ((), (), s32[]{:S(2)}) async-start(), calls=%async_computation.5 | async-start | bytes 589824 | tf_op jit(solution)/shard_map/reduce_scatter | solution.py:151
  69.2 204.7 %reduce-scatter.13.cloned.1.call-start = ((), (), s32[]{:S(2)}) async-start(), calls=%async_computation.8 | async-start | bytes 10616832
  122.9 23.2 %copy-start.6 = (f32[3072]{0:T(1024)S(1)}, f32[3072]{0:T(1024)}, u32[]{:S(2)}) copy-start(f32[3072]{0:T(1024)} %param.28) | copy-start | bytes 36868
  122.9 26.5 %copy-start.7 = (f32[3072]{0:T(1024)S(1)}, f32[3072]{0:T(1024)}, u32[]{:S(2)}) copy-start(f32[3072]{0:T(1024)} %param.29) | copy-start | bytes 36868
  122.9 26.5 %copy-start.10 = (f32[3072]{0:T(1024)S(1)}, f32[3072]{0:T(1024)}, u32[]{:S(2)}) copy-start(f32[3072]{0:T(1024)} %param.30) | copy-start | bytes 36868
  198.5 155.6 %reduce-scatter.11.cloned.1.call-start = ((), (), s32[]{:S(2)}) async-start(), calls=%async_computation.7 | async-start | bytes 10616832 | tf_op jit(solution)/shard_map/reduce_scatter | solution.py:145
  204.8 1.8 copy-start
  212.9 0.8 copy-start.2
  212.9 0.9 copy-start.4
  212.9 1.8 copy-start.3
Sparse Core Ops, SparseCore 0:
  60.6 18.9 reduce-scatter.6
  81.7 35.2 all-gather.2
  120.7 32.9 reduce-scatter.8
  198.6 75.2 reduce-scatter.12
  277.3 76.8 reduce-scatter.10
where the time goes:
time: 365 us; the launch traced here: 364 us
  waiting for transfers between devices  180 us (49%)
  blocking collectives  71.3 us (20%)
  matrix products  45.1 us (12%)
  other arithmetic  25.8 us (7%)
  local copies, waits for them, and re-layouts  20.9 us (6%)
  between operations  20 us (5%)
    reduce_scatter x1, waiting for transfers between devices, on_device(): lax.psum_scatter(up_part.astype(jnp.bfloat16), 'dp', scatter_dimension=0,...  76.9 us
    unnamed x6, waiting for transfers between devices  56.6 us
    all_gather x1, waiting for transfers between devices, on_device(): lax.all_gather(normed, 'fsdp', axis=0, tiled=True)  36.6 us
    unnamed x3, blocking collectives  34.8 us
    unnamed x30, local copies, waits for them, and re-layouts  20.4 us
    all_gather x1, blocking collectives, on_device(): lax.all_gather(img_b, 'fsdp', axis=0, tiled=True)  14.2 us
    all_gather x1, blocking collectives, on_device(): group_grad = lax.all_gather(grad_row, 'fsdp', axis=0, tiled=True)  13.3 us
    reduce_scatter x1, waiting for transfers between devices, on_device(): lax.psum_scatter(image_acc.astype(jnp.bfloat16), 'fsdp', scatter_dimensio...  10.2 us
  transfers between devices with their start and end apart: 5, of which 4 were waited for; matrix products, arithmetic and copies ran while one was open for 21% of the time, Pallas kernels for 0%

commit v1 on v0

--- a/solution.py
+++ b/solution.py
@@ -5,6 +5,28 @@
 
 KERNEL = 7
 SIDE = 8
+
+
+def laid_out(pieces, dim):
+    shape = list(pieces.shape[1:])
+    shape[dim] *= pieces.shape[0]
+    return jnp.moveaxis(pieces, 0, dim).reshape(shape)
+
+
+def collect(x, axis, dim):
+    size = lax.axis_size(axis)
+    pairs = [(i, (i + 1) % size) for i in range(size)]
+    back = [(b, a) for a, b in pairs]
+    lower, upper = ([], [])
+    for step in range(size - 1):
+        if step % 2 == 0:
+            lower.append(lax.ppermute(lower[-1] if lower else x, axis, pairs))
+        else:
+            upper.append(lax.ppermute(upper[-1] if upper else x, axis, back))
+    blocks = jnp.stack([*lower[::-1], x, *upper])
+    shift = lax.axis_index(axis) - len(lower)
+    blocks = blocks[(jnp.arange(size) - shift) % size]
+    return laid_out(blocks, dim)
 
 
 def unit_rows(matrix):
@@ -99,7 +121,7 @@
     group_img, group_ids, group_normed = (
         lax.all_gather(img_b, "fsdp", axis=0, tiled=True),
         lax.all_gather(img_ids, "fsdp", axis=0, tiled=True),
-        lax.all_gather(normed, "fsdp", axis=0, tiled=True),
+        collect(normed, "fsdp", 0),
     )
     image_count = group_normed.shape[0] // (SIDE * SIDE)
     image_part, text_part = pair_tile(

time: 365 us -> 354 us (0.970)
  waiting for transfers between devices: 180 us -> 165 us
  starting transfers between devices: 0.2 us -> 4.03 us
    all_gather x1 -> x0, waiting for transfers between devices: 36.6 us -> none  [on_device(): lax.all_gather(normed, 'fsdp', axis=0, tiled=True)]
    ppermute x0 -> x3, waiting for transfers between devices: none -> 29.5 us  [the longest x2 29.5 us: collect(): lower.append(lax.ppermute(lower[-1] if lower else x, axis, pairs))]
    reduce_scatter x1, waiting for transfers between devices: 10.2 us -> 0.02 us  [on_device(): lax.psum_scatter(image_acc.astype(jnp.bfloat16), 'fsdp', scatter_dimensio...]
    ppermute x0 -> x3, starting transfers between devices: none -> 3.86 us  [the longest x1 2.3 us: collect(): upper.append(lax.ppermute(upper[-1] if upper else x, axis, back))]
    unnamed x6 -> x5, waiting for transfers between devices: 56.6 us -> 58.2 us
    unnamed x30 -> x36, local copies, waits for them, and re-layouts: 20.4 us -> 19.7 us
  transfers between devices with their start and end apart: 5 -> 7, of which waited for: 4 -> 4; matrix products, arithmetic and copies ran while one was open for 21% -> 23% of each run, Pallas kernels for 0% -> 0%
where the time goes in v1:
time: 354 us; the launch traced here: 353 us
  waiting for transfers between devices  165 us (47%)
  blocking collectives  70.2 us (20%)
  matrix products  44.8 us (13%)
  other arithmetic  26.6 us (8%)
  local copies, waits for them, and re-layouts  22.4 us (6%)
  between operations  20.1 us (6%)
  starting transfers between devices  4.03 us (1%)
    reduce_scatter x1, waiting for transfers between devices, on_device(): lax.psum_scatter(up_part.astype(jnp.bfloat16), 'dp', scatter_dimension=0,...  76.9 us
    unnamed x5, waiting for transfers between devices  58.2 us
    unnamed x3, blocking collectives  33.9 us
    ppermute x2, waiting for transfers between devices, collect(): lower.append(lax.ppermute(lower[-1] if lower else x, axis, pairs))  29.5 us
    unnamed x36, local copies, waits for them, and re-layouts  19.7 us
    all_gather x1, blocking collectives, on_device(): lax.all_gather(img_b, 'fsdp', axis=0, tiled=True)  14.2 us
    all_gather x1, blocking collectives, on_device(): group_grad = lax.all_gather(grad_row, 'fsdp', axis=0, tiled=True)  13.1 us
    dot_general x1, matrix products, on_device(): jnp.dot(active_total.T, group_grad.astype(jnp.float32), precision=lax.Pre...  9.72 us
  transfers between devices with their start and end apart: 7, of which 4 were waited for; matrix products, arithmetic and copies ran while one was open for 23% of the time, Pallas kernels for 0%

profile of v1, /device:TPU:0, one launch (start us, length us, event | category | flops | bytes accessed | tf_op | source)
XLA Modules:
  0.0 352.7 jit_solution(15808672135546497126)
XLA Ops:
  15.3 9.9 %all-reduce.1 = s32[128]{0:T(128)S(1)} all-reduce(s32[128]{0:T(128)S(1)} %dynamic-update-slice), channel_id=1, replica_groups=mesh['dp'=8,'fsdp'=4] {'fsdp'}, use_global_device_ids=true, to_apply=%add.1 | all-reduce | flops 128 | bytes 1024
  26.1 8.0 %all-reduce.2 = s32[256]{0:T(256)S(1)} all-reduce(s32[256]{0:T(256)S(1)} %dynamic-update-slice.1), channel_id=1, replica_groups=mesh['dp'=8,'fsdp'=4] {'dp'}, use_global_device_ids=true, to_apply=%add.2 | all-reduce | flops 256 | bytes 2048
  35.9 14.2 %all_gather.17 = bf16[128,1024]{1,0:T(8,128)(2,1)S(1)} all-gather(bf16[32,1024]{1,0:T(8,128)(2,1)S(1)} %fusion.151), channel_id=1, replica_groups=mesh['dp'=8,'fsdp'=4] {'fsdp'}, dimensions={0}, use_global_device_ids=true | all-gather | bytes 327680 | tf_op jit(solution)/shard_map/all_gather | solution.py:122
  50.2 9.0 %all_gather.18 = bf16[256,1024]{1,0:T(8,128)(2,1)S(1)} all-gather(bf16[32,1024]{1,0:T(8,128)(2,1)S(1)} %fusion.152), channel_id=1, replica_groups=mesh['dp'=8,'fsdp'=4] {'dp'}, dimensions={0}, use_global_device_ids=true | all-gather | bytes 589824 | tf_op jit(solution)/shard_map/all_gather | solution.py:130
  61.1 5.5 %fusion.156 = (f32[8,8]{1,0:T(8,128)S(1)}, f32[1,8,8,3072]{3,2,1,0:T(8,128)S(1)}) fusion(f32[3072]{0:T(1024)S(1)} %bitcast.161, f32[3072]{0:T(1024)S(1)} %bitcast.162, f32[3072]{0:T(1024)S(1)} %bitcast.165, f32[3072]{0:T(1024)S(1)} %bitcast.166, f32[3072]{0:T(1024)S(1)} %bitcast.167, f32[3072]{0:T(1024)S(1)} %bitcast.168, f32[3072]{0:T(1024)S(1)} %bitcast.169, ...), kind=kLoop, calls=%fused_computation.250 | loop fusion | flops 19267520 | bytes 2175232 | tf_op jit(solution)/shard_map/reduce_sum | solution.py:68
  67.2 2.3 collective-permute-start.2
  70.9 19.5 %collective-permute-done = bf16[64,3072]{1,0:T(8,128)(2,1)S(1)} collective-permute-done((bf16[64,3072]{1,0:T(8,128)(2,1)S(1)}, bf16[64,3072]{1,0:T(8,128)(2,1)S(1)}, u32[]{:S(2)}, u32[]{:S(2)}) %collective-permute-start) | collective-permute-done | bytes 393248 | tf_op jit(solution)/shard_map/ppermute | solution.py:23
  92.9 10.0 %collective-permute-done.1 = bf16[64,3072]{1,0:T(8,128)(2,1)S(1)} collective-permute-done((bf16[64,3072]{1,0:T(8,128)(2,1)S(1)}, bf16[64,3072]{1,0:T(8,128)(2,1)S(1)}, u32[]{:S(2)}, u32[]{:S(2)}) %collective-permute-start.1) | collective-permute-done | bytes 393248 | tf_op jit(solution)/shard_map/ppermute | solution.py:23
  104.3 2.1 gather_fusion
  106.5 7.8 %convert_reduce_fusion = (f32[4,1536]{1,0:T(4,128)S(1)}, f32[256,1536]{1,0:T(8,128)}) fusion(bf16[256,3072]{1,0:T(8,128)(2,1)S(1)} %bitcast.142, bf16[3072,1536]{1,0:T(8,128)(2,1)} %param.26), kind=kOutput, calls=%fused_computation.67 | convolution fusion | flops 2420238336 | bytes 12607488 | tf_op jit(solution)/shard_map/dot_general | solution.py:137
  114.4 3.8 %convolution_convert_fusion.2 = bf16[4,3072]{1,0:T(4,128)(2,1)S(1)} fusion(bf16[1536,3072]{1,0:T(8,128)(2,1)S(1)} %bitcast.140, f32[4,1536]{1,0:T(4,128)S(1)} %get-tuple-element.61), kind=kOutput, calls=%fused_computation.51 | convolution fusion | flops 226510848 | bytes 9486336 | tf_op jit(solution)/shard_map/dot_general | solution.py:143
  118.2 15.9 %all-reduce.3 = bf16[4,3072]{1,0:T(4,128)(2,1)S(1)} all-reduce(bf16[4,3072]{1,0:T(4,128)(2,1)S(1)} %convolution_convert_fusion.2), channel_id=4, replica_groups=mesh['dp'=8,'fsdp'=4] {'fsdp'}, use_global_device_ids=true, to_apply=%region_10.11.clone | all-reduce | flops 12288 | bytes 49152
  137.4 3.7 %fusion.130 = f32[1,1024]{1,0:T(1,128)S(1)} fusion(bf16[3072,1024]{1,0:T(8,128)(2,1)} %param.31, f32[1,3072]{1,0:T(1,128)S(1)} %bitcast.209, f32[1,3072]{1,0:T(1,128)S(1)} %bitcast.206, f32[1,3072]{1,0:T(1,128)S(1)} %get-tuple-element.7, f32[]{:T(128)S(6)} %sqrt.32, f32[]{:T(128)S(6)} %div.98), kind=kOutput, calls=%fused_computation.205 | convolution fusion | flops 6306816 | bytes 6332424 | tf_op jit(solution)/shard_map/dot_general | solution.py:78
  143.7 4.5 %fusion.141 = f32[1,3072]{1,0:T(1,128)S(1)} fusion(bf16[3072,1024]{1,0:T(8,128)(2,1)} %param.31, f32[1,1024]{1,0:T(1,128)S(1)} %bitcast.207, f32[32,1024]{1,0:T(8,128)S(1)} %convert_element_type.114, f32[]{:T(128)S(6)} %sqrt.33), kind=kOutput, calls=%fused_computation.224 | convolution fusion | flops 6294528 | bytes 6311940 | tf_op jit(solution)/shard_map/dot_general | solution.py:81
  150.8 13.1 %all-gather = bf16[4,1,3072]{2,1,0:T(2,128)(2,1)S(1)} all-gather(bf16[1,1,3072]{2,1,0:T(2,128)(2,1)S(1)} %convert_bitcast_fusion.1), channel_id=1, replica_groups=mesh['dp'=8,'fsdp'=4] {'fsdp'}, dimensions={0}, use_global_device_ids=true | all-gather | bytes 30720 | tf_op jit(solution)/shard_map/all_gather | solution.py:155
  163.9 9.7 %convolution_convert_fusion = bf16[1536,3072]{1,0:T(8,128)(2,1)} fusion(f32[4,1536]{1,0:T(4,128)S(1)} %get-tuple-element.61, bf16[4,1,3072]{2,1,0:T(2,128)(2,1)S(1)} %all-gather), kind=kOutput, calls=%fused_computation.49 | convolution fusion | flops 231211008 | bytes 9486336 | tf_op jit(solution)/shard_map/dot_general | solution.py:162
  173.6 12.7 %copy.20 = bf16[1536,3072]{0,1:T(8,128)(2,1)} copy(bf16[1536,3072]{1,0:T(8,128)(2,1)} %convolution_convert_fusion) | data formatting | bytes 18874368
  186.4 6.3 %fusion.127 = f32[4,1536]{1,0:T(4,128)S(1)} fusion(bf16[1536,3072]{1,0:T(8,128)(2,1)} %param.27, bf16[4,1,3072]{2,1,0:T(2,128)(2,1)S(1)} %all-gather), kind=kOutput, calls=%fused_computation.202 | convolution fusion | flops 37748736 | bytes 9486336 | tf_op jit(solution)/shard_map/dot_general | solution.py:156
  193.8 6.5 %convolution_convert_fusion.1 = bf16[3072,1536]{1,0:T(8,128)(2,1)} fusion(bf16[256,3072]{1,0:T(8,128)(2,1)S(1)} %bitcast.143, bf16[256,1536]{1,0:T(8,128)(2,1)S(1)} %fusion.6), kind=kOutput, calls=%fused_computation.50 | convolution fusion | flops 2420637696 | bytes 11796480 | tf_op jit(solution)/shard_map/dot_general | solution.py:165
  203.3 1.6 fusion.125
  204.9 58.1 %reduce-scatter.13.cloned.1.call-done = bf16[384,1536]{1,0:T(8,128)(2,1)} async-done(((bf16[3072,1536]{1,0:T(8,128)(2,1)}), bf16[384,1536]{1,0:T(8,128)(2,1)}) %reduce-scatter.13.cloned.1.call-update) | async-done | bytes 1179664
  263.0 1.7 copy.21
  266.3 76.9 %reduce-scatter.11.cloned.1.call-done = bf16[384,1536]{1,0:T(8,128)(2,1)} async-done(((bf16[3072,1536]{1,0:T(8,128)(2,1)}), bf16[384,1536]{1,0:T(8,128)(2,1)}) %reduce-scatter.11.cloned.1.call-update) | async-done | bytes 1179664 | tf_op jit(solution)/shard_map/reduce_scatter | solution.py:167
  343.2 3.0 convert_element_type.131
  (89 shorter events, 26.6 us)
Async XLA Ops:
  7.2 84.9 %reduce-scatter.7.cloned.1.call-start = ((), (), s32[]{:S(2)}) async-start(), calls=%async_computation.4 | async-start | bytes 327680 | tf_op jit(solution)/shard_map/reduce_scatter | solution.py:145
  50.2 10.4 %copy-start.5 = (f32[49,3072]{1,0:T(8,128)S(1)}, f32[49,3072]{1,0:T(8,128)}, u32[]{:S(2)}) copy-start(f32[49,3072]{1,0:T(8,128)} %param.23) | copy-start | bytes 1806340
  59.2 1.8 copy-start.1
  60.5 141.7 %reduce-scatter.9.cloned.1.call-start = ((), (), s32[]{:S(2)}) async-start(), calls=%async_computation.5 | async-start | bytes 589824 | tf_op jit(solution)/shard_map/reduce_scatter | solution.py:173
  61.1 6.0 %copy-start.6 = (f32[3072]{0:T(1024)S(1)}, f32[3072]{0:T(1024)}, u32[]{:S(2)}) copy-start(f32[3072]{0:T(1024)} %param.25) | copy-start | bytes 36868
  61.1 6.0 %copy-start.7 = (f32[3072]{0:T(1024)S(1)}, f32[3072]{0:T(1024)}, u32[]{:S(2)}) copy-start(f32[3072]{0:T(1024)} %param.24) | copy-start | bytes 36868
  67.2 25.7 %collective-permute-start.2 = (bf16[64,3072]{1,0:T(8,128)(2,1)S(1)}, bf16[64,3072]{1,0:T(8,128)(2,1)S(1)}, u32[]{:S(2)}, u32[]{:S(2)}) collective-permute-start(bf16[64,3072]{1,0:T(8,128)(2,1)S(1)} %fusion.121), channel_id=1, source_target_pairs={{1,0},{2,1},{3,2},{0,3},{5,4},{6,5},{7,6},{4,7},{9,8},{10,9},{11,1... | collective-permute-start | bytes 1179656 | tf_op jit(solution)/shard_map/ppermute | solution.py:25
  69.5 20.9 %collective-permute-start = (bf16[64,3072]{1,0:T(8,128)(2,1)S(1)}, bf16[64,3072]{1,0:T(8,128)(2,1)S(1)}, u32[]{:S(2)}, u32[]{:S(2)}) collective-permute-start(bf16[64,3072]{1,0:T(8,128)(2,1)S(1)} %fusion.121), channel_id=1, source_target_pairs={{0,1},{1,2},{2,3},{3,0},{4,5},{5,6},{6,7},{7,4},{8,9},{9,10},{10,1... | collective-permute-start | bytes 1179656 | tf_op jit(solution)/shard_map/ppermute | solution.py:23
  70.7 192.3 %reduce-scatter.13.cloned.1.call-start = ((), (), s32[]{:S(2)}) async-start(), calls=%async_computation.7 | async-start | bytes 10616832
  90.4 12.6 %collective-permute-start.1 = (bf16[64,3072]{1,0:T(8,128)(2,1)S(1)}, bf16[64,3072]{1,0:T(8,128)(2,1)S(1)}, u32[]{:S(2)}, u32[]{:S(2)}) collective-permute-start(bf16[64,3072]{1,0:T(8,128)(2,1)S(1)} %collective-permute-done), channel_id=1, source_target_pairs={{0,1},{1,2},{2,3},{3,0},{4,5},{5,6},{6,7},{7,4},{8,9},{9,10},{10,1... | collective-permute-start | bytes 1179656 | tf_op jit(solution)/shard_map/ppermute | solution.py:23
  104.3 10.0 %slice-start = ((s8[9437184]{0:T(1024)(128)(4,1)}), s8[1048576]{0:T(1024)(128)(4,1)S(1)}, s32[]{:S(2)}) async-start(s8[9437184]{0:T(1024)(128)(4,1)} %bitcast.139), calls=%async_computation.8 | async-start | bytes 2097152
  106.5 7.9 %slice-start.1 = ((s8[9437184]{0:T(1024)(128)(4,1)}), s8[4194304]{0:T(1024)(128)(4,1)S(1)}, s32[]{:S(2)}) async-start(s8[9437184]{0:T(1024)(128)(4,1)} %bitcast.139), calls=%async_computation.9 | async-start | bytes 8388608
  106.5 7.9 %slice-start.2 = ((s8[9437184]{0:T(1024)(128)(4,1)}), s8[4194304]{0:T(1024)(128)(4,1)S(1)}, s32[]{:S(2)}) async-start(s8[9437184]{0:T(1024)(128)(4,1)} %bitcast.139), calls=%async_computation.10 | async-start | bytes 8388608
  114.4 19.7 %copy-start.8 = (f32[3072]{0:T(1024)S(1)}, f32[3072]{0:T(1024)}, u32[]{:S(2)}) copy-start(f32[3072]{0:T(1024)} %param.28) | copy-start | bytes 36868
  114.4 23.0 %copy-start.9 = (f32[3072]{0:T(1024)S(1)}, f32[3072]{0:T(1024)}, u32[]{:S(2)}) copy-start(f32[3072]{0:T(1024)} %param.29) | copy-start | bytes 36868
  114.4 23.0 %copy-start.10 = (f32[3072]{0:T(1024)S(1)}, f32[3072]{0:T(1024)}, u32[]{:S(2)}) copy-start(f32[3072]{0:T(1024)} %param.30) | copy-start | bytes 36868
  186.4 156.8 %reduce-scatter.11.cloned.1.call-start = ((), (), s32[]{:S(2)}) async-start(), calls=%async_computation.6 | async-start | bytes 10616832 | tf_op jit(solution)/shard_map/reduce_scatter | solution.py:167
  186.4 6.3 %copy-start = (f32[256,1536]{1,0:T(8,128)S(1)}, f32[256,1536]{1,0:T(8,128)}, u32[]{:S(2)}) copy-start(f32[256,1536]{1,0:T(8,128)} %get-tuple-element.62) | copy-start | bytes 4718596
  200.4 0.9 copy-start.2
  200.4 0.9 copy-start.4
  200.4 1.9 copy-start.3
Sparse Core Ops, SparseCore 0:
  60.6 20.6 reduce-scatter.6
  84.9 38.1 reduce-scatter.8
  186.5 76.4 reduce-scatter.12
  266.3 76.8 reduce-scatter.10
